TPU v7x, 32 devices: a whole 2x2x4 slice. The times are simulated.
32 devices in a mesh: rows: 4 (over x, core), filt: 8 (over z, y).
Axes of the slice: x: 2, y: 2, z: 4, core: 2. Of those that a mesh axis runs over, the one named last changes fastest.
Arguments:
- inputs: bfloat16 [1024, 16, 512], P('filt', 'rows'), may hold values from -6 to 6
- filters: float32 [24, 1024], replicated, may hold values from -0.1875 to 0.1875
- gain_in: float32 [512], replicated, may hold values from 0.5 to 1.5
- mixing: bfloat16 [48, 512, 512], P('filt'), may hold values from -0.0390625 to 0.0390625
- regression: bfloat16 [3, 512, 512], replicated, may hold values from -0.15625 to 0.15625
- gain_mid: float32 [512], replicated, may hold values from 0.5 to 1.5
- w_gate: bfloat16 [512, 2048], P(None, 'filt'), may hold values from -0.25 to 0.25
- w_up: bfloat16 [512, 2048], P(None, 'filt'), may hold values from -0.25 to 0.25
- w_down: bfloat16 [2048, 512], P('filt'), may hold values from -0.1875 to 0.1875
- out_grad: bfloat16 [1024, 16, 512], P('filt', 'rows'), may hold values from -6 to 6
Outputs:
- block_out: bfloat16 [1024, 16, 512], P('filt', 'rows')
- input_grad: float32 [1024, 16, 512], P('filt', 'rows')
- mixing_grad: float32 [48, 512, 512], P('filt')
- regression_grad: float32 [3, 512, 512], replicated
- gain_in_grad: float32 [512], replicated
- gain_mid_grad: float32 [512], replicated
- w_gate_grad: float32 [512, 2048], P(None, 'filt')
- w_up_grad: float32 [512, 2048], P(None, 'filt')
- w_down_grad: float32 [2048, 512], P('filt')
All inputs are finite; a program needn't handle non-finite values.
Results may differ from a plain program's by a relative error of at most 0.013.
Values may be sent and summed in bfloat16 or wider, within the bound.
No kernel may reach another device: no remote copies, remote signals or barrier semaphores. Data moves between devices by JAX's collectives and lax.ppermute only.
A program may use at most 256 MiB of HBM per device.

v0:
```python
import jax
import jax.numpy as jnp
from jax import lax
from jax.sharding import PartitionSpec as P

epsilon = 1e-05


def normalize(values, gain):
    factor = lax.rsqrt(jnp.mean(values * values, axis=-1, keepdims=True) + epsilon)
    normed = values * factor
    return (normed, factor, normed * gain)


def norm_backward(grad_out, normed, factor, gain):
    inner_grad = grad_out * gain
    return factor * (inner_grad - normed * jnp.mean(inner_grad * normed, axis=-1, keepdims=True))


def contract_rows(left, right):
    return lax.dot_general(
        left, right, (((0,), (0,)), ((), ())), preferred_element_type=jnp.float32
    )


def times_transpose(left, right):
    return lax.dot_general(
        left, right, (((1,), (1,)), ((), ())), preferred_element_type=jnp.float32
    )


def activation_grads(gate_pre, up_values, grad_hidden):
    sigmoid_value = jax.nn.sigmoid(gate_pre)
    slope = sigmoid_value * (1.0 + gate_pre * (1.0 - sigmoid_value))
    gate_back = (grad_hidden * up_values * slope).astype(jnp.bfloat16)
    up_back = (grad_hidden * gate_pre * sigmoid_value).astype(jnp.bfloat16)
    return (gate_back, up_back)


def upper_toeplitz(kernel_row):
    seq_length = kernel_row.shape[0]
    padded = jnp.concatenate([kernel_row, jnp.zeros((seq_length,), kernel_row.dtype)])
    tiled = jnp.tile(padded, seq_length)[: seq_length * (2 * seq_length - 1)]
    return tiled.reshape(seq_length, 2 * seq_length - 1)[:, :seq_length]


def kernel_matrix(filters, global_branch):
    seq_length = filters.shape[1]
    alternate = jnp.where(jnp.arange(seq_length) % 2 == 0, 1.0, -1.0).astype(jnp.float32)
    kernel_row = lax.dynamic_slice_in_dim(filters, global_branch // 2, 1, 0)[0]
    kernel_row = jnp.where(global_branch % 2 == 1, kernel_row * alternate, kernel_row)
    return upper_toeplitz(kernel_row.astype(jnp.bfloat16))


def shards(inputs, filters, gain_in, mixing, regression, gain_mid, w_gate, w_up, w_down, out_grad):
    shard_rows, local_seqs, model_width = inputs.shape
    group_count = lax.axis_size("filt")
    seq_length = shard_rows * group_count
    branches = mixing.shape[0]
    lag_count = regression.shape[0]
    row_width = local_seqs * model_width
    own_start = lax.axis_index("filt") * shard_rows
    residual = inputs.astype(jnp.float32)
    normed_in, factor_in, scaled_in = normalize(residual, gain_in)
    states = lax.all_gather(scaled_in.astype(jnp.bfloat16), "filt", axis=0, tiled=True)
    states_rows = states.reshape(seq_length * local_seqs, model_width)
    toeplitz = [
        kernel_matrix(filters, lax.axis_index("filt") * branches + branch)
        for branch in range(branches)
    ]
    projected = [
        jnp.dot(states_rows, mixing[branch], preferred_element_type=jnp.float32)
        .astype(jnp.bfloat16)
        .reshape(seq_length, row_width)
        for branch in range(branches)
    ]
    row_count = lax.axis_size("filt") * shard_rows
    summed = jnp.zeros((row_count, row_width), jnp.float32)
    for project_branch in range(branches):
        slab = toeplitz[project_branch]
        summed = summed + jnp.einsum(
            "ut,un->tn", slab, projected[project_branch], preferred_element_type=jnp.float32
        )
    spectral = lax.psum_scatter(
        summed.reshape(row_count, local_seqs, model_width), "filt", scatter_dimension=0, tiled=True
    )
    padded_states = jnp.concatenate(
        [jnp.zeros((lag_count - 1, local_seqs, model_width), jnp.bfloat16), states], axis=0
    )
    lagged = jnp.stack(
        [
            lax.dynamic_slice_in_dim(
                padded_states, own_start + lag_count - 1 - lag_index, shard_rows, 0
            )
            for lag_index in range(lag_count)
        ]
    )
    regress = jnp.einsum("itsd,ide->tse", lagged, regression, preferred_element_type=jnp.float32)
    middle = residual + spectral + regress
    normed_mid, factor_mid, scaled_mid = normalize(middle, gain_mid)
    middle_low = scaled_mid.astype(jnp.bfloat16)
    middle_all = lax.all_gather(middle_low, "filt", axis=0, tiled=True).reshape(
        seq_length * local_seqs, model_width
    )
    gate_pre = jnp.dot(middle_all, w_gate, preferred_element_type=jnp.float32)
    up_values = jnp.dot(middle_all, w_up, preferred_element_type=jnp.float32)
    hidden = (jax.nn.silu(gate_pre) * up_values).astype(jnp.bfloat16)
    hidden_rows = hidden.reshape(seq_length, local_seqs, hidden.shape[1])
    row_count = shard_rows * lax.axis_size("filt")
    slab = hidden_rows.reshape(row_count * local_seqs, -1)
    block_value = middle + lax.psum_scatter(
        jnp.dot(slab, w_down, preferred_element_type=jnp.float32)
        .reshape(row_count, local_seqs, model_width)
        .astype(jnp.bfloat16),
        "filt",
        scatter_dimension=0,
        tiled=True,
    ).astype(jnp.float32)
    grad_all = lax.all_gather(out_grad, "filt", axis=0, tiled=True).reshape(
        seq_length * local_seqs, model_width
    )
    down_partial = contract_rows(hidden, grad_all)
    grad_hidden = times_transpose(grad_all, w_down)
    gate_back, up_back = activation_grads(gate_pre, up_values, grad_hidden)
    gate_partial = contract_rows(middle_all, gate_back)
    up_partial = contract_rows(middle_all, up_back)
    gate_rows = gate_back.reshape(seq_length, local_seqs, -1)
    up_rows = up_back.reshape(seq_length, local_seqs, -1)
    row_count = lax.axis_size("filt") * shard_rows
    gate_slab = gate_rows.reshape(row_count * local_seqs, -1)
    up_slab = up_rows.reshape(row_count * local_seqs, -1)
    summed = times_transpose(gate_slab, w_gate) + times_transpose(up_slab, w_up)
    mid_back = lax.psum_scatter(
        summed.reshape(row_count, local_seqs, model_width), "filt", scatter_dimension=0, tiled=True
    )
    gain_mid_part = jnp.sum(mid_back * normed_mid, axis=(0, 1))
    middle_grad = out_grad.astype(jnp.float32) + norm_backward(
        mid_back, normed_mid, factor_mid, gain_mid
    )
    mix_back = middle_grad.astype(jnp.bfloat16)
    mix_all = lax.all_gather(mix_back, "filt", axis=0, tiled=True).reshape(seq_length, row_width)
    proj_back = [
        jnp.dot(toeplitz[branch], mix_all, preferred_element_type=jnp.float32).astype(jnp.bfloat16)
        for branch in range(branches)
    ]
    mixing_part = jnp.stack(
        [
            contract_rows(
                states_rows, proj_back[branch].reshape(seq_length * local_seqs, model_width)
            )
            for branch in range(branches)
        ]
    )
    lag_terms = jnp.einsum(
        "tse,ide->itsd", mix_back, regression, preferred_element_type=jnp.float32
    )
    regression_part = jnp.einsum(
        "itsd,tse->ide", lagged, mix_back, preferred_element_type=jnp.float32
    )
    spread = jnp.zeros((seq_length + lag_count - 1, local_seqs, model_width), jnp.float32)
    for lag_index in range(lag_count):
        begin = own_start + lag_count - 1 - lag_index
        current = lax.dynamic_slice_in_dim(spread, begin, shard_rows, 0)
        spread = lax.dynamic_update_slice_in_dim(spread, current + lag_terms[lag_index], begin, 0)
    spread = spread[lag_count - 1 :]
    row_count = lax.axis_size("filt") * shard_rows
    summed = spread.reshape(row_count * local_seqs, model_width)
    for branch in range(branches):
        slab = proj_back[branch]
        summed = summed + times_transpose(
            slab.reshape(row_count * local_seqs, model_width), mixing[branch]
        )
    state_back = lax.psum_scatter(
        summed.reshape(row_count, local_seqs, model_width), "filt", scatter_dimension=0, tiled=True
    )
    gain_in_part = jnp.sum(state_back * normed_in, axis=(0, 1))
    input_grad = middle_grad + norm_backward(state_back, normed_in, factor_in, gain_in)
    mixing_grad, w_gate_grad, w_up_grad, w_down_grad = (
        lax.psum(mixing_part.astype(jnp.bfloat16), "rows").astype(jnp.float32),
        lax.psum(gate_partial.astype(jnp.bfloat16), "rows").astype(jnp.float32),
        lax.psum(up_partial.astype(jnp.bfloat16), "rows").astype(jnp.float32),
        lax.psum(down_partial.astype(jnp.bfloat16), "rows").astype(jnp.float32),
    )
    regression_grad, gain_in_grad, gain_mid_grad = lax.psum(
        (regression_part, gain_in_part, gain_mid_part), ("rows", "filt")
    )
    return (
        block_value.astype(jnp.bfloat16),
        input_grad,
        mixing_grad,
        regression_grad,
        gain_in_grad,
        gain_mid_grad,
        w_gate_grad,
        w_up_grad,
        w_down_grad,
    )


def solution(mesh):
    placed = (
        P("filt", "rows", None),
        P(),
        P(),
        P("filt", None, None),
        P(),
        P(),
        P(None, "filt"),
        P(None, "filt"),
        P("filt", None),
        P("filt", "rows", None),
    )
    return jax.shard_map(
        shards,
        mesh=mesh,
        in_specs=placed,
        out_specs=(
            P("filt", "rows", None),
            P("filt", "rows", None),
            P("filt", None, None),
            P(),
            P(),
            P(),
            P(None, "filt"),
            P(None, "filt"),
            P("filt", None),
        ),
        check_vma=False,
    )
```

profile of v0, /device:TPU:0, one launch (start us, length us, event | category | flops | bytes accessed | tf_op | source)
XLA Modules:
  0.0 1469.2 jit_solution(7512996835774549502)
XLA Ops:
  17.1 10.8 reshape.145
  32.7 10.8 reshape.141
  48.4 10.7 reshape.136
  64.2 10.7 reshape.139
  79.6 10.7 reshape.147
  95.2 10.7 reshape.143
  194.7 10.8 fusion.3
  233.1 24.2 %add_add_fusion.1 = f32[1024,2048]{1,0:T(8,128)} fusion(f32[1024,2048]{1,0:T(8,128)} %fusion.3, f32[1024,2048]{1,0:T(8,128)} %fusion.6, f32[1024,2048]{1,0:T(8,128)} %fusion.9, f32[1024,2048]{1,0:T(8,128)} %fusion.15, f32[1024,2048]{1,0:T(8,128)} %fusion.12, bf16[1024,2048]{1,0:T(8,128)(2,1)} %reshape.148, bf16[1024,2047]{1,0:T(8,128)(2,1)} %reshape.147), kind=kOutput, calls=%fused_computation.2 | convolution fusion | flops 4305453056 | bytes 56623104 | tf_op jit(solution)/shard_map/ut,un->tn/dot_general | solution.py:81
  269.0 148.6 %reduce-scatter.5.cloned.1.call-done = f32[128,4,512]{2,0,1:T(8,128)} async-done(((f32[1024,4,512]{2,0,1:T(8,128)}), f32[128,4,512]{2,0,1:T(8,128)}) %reduce-scatter.5.cloned.1.call-update) | async-done | bytes 1048592 | tf_op jit(solution)/shard_map/reduce_scatter | solution.py:84
  421.7 70.7 %all-gather.9.cloned.1.call-done = bf16[1024,4,512]{2,1,0:T(4,128)(2,1)} async-done(((bf16[128,4,512]{2,1,0:T(4,128)(2,1)}), bf16[1024,4,512]{2,1,0:T(4,128)(2,1)}) %all-gather.9.cloned.1.call-update) | async-done | bytes 4194320 | tf_op jit(solution)/shard_map/all_gather | solution.py:119
  499.7 67.2 %all-gather.7.cloned.1.call-done = bf16[1024,4,512]{2,0,1:T(8,128)(2,1)} async-done(((bf16[128,4,512]{2,0,1:T(8,128)(2,1)}), bf16[1024,4,512]{2,0,1:T(8,128)(2,1)}) %all-gather.7.cloned.1.call-update) | async-done | bytes 4194320 | tf_op jit(solution)/shard_map/all_gather | solution.py:102
  597.6 10.0 reshape.152
  617.0 147.7 %reduce-scatter.9.cloned.1.call-done = f32[128,4,512]{2,0,1:T(8,128)} async-done(((f32[1024,4,512]{2,0,1:T(8,128)}), f32[128,4,512]{2,0,1:T(8,128)}) %reduce-scatter.9.cloned.1.call-update) | async-done | bytes 1048592 | tf_op jit(solution)/shard_map/reduce_scatter | solution.py:133
  815.6 12.1 copy.51
  827.8 10.1 reshape.153
  848.8 9.5 convolution_convert_fusion.7
  990.3 22.8 %add_add_fusion = f32[4096,512]{1,0:T(8,128)} fusion(f32[4096,512]{1,0:T(8,128)} %fusion.55, f32[4096,512]{1,0:T(8,128)} %fusion.58, f32[4096,512]{1,0:T(8,128)} %fusion.61, f32[4096,512]{1,0:T(8,128)} %fusion.64, f32[4096,512]{1,0:T(8,128)} %reshape.153, f32[4096,512]{1,0:T(8,128)} %fusion.67, bf16[4096,512]{1,0:T(8,128)(2,1)} %reshape.160, ...), kind=kOutput, calls=%fused_computation.1 | convolution fusion | flops 2160066560 | bytes 63438848 | tf_op jit(solution)/shard_map/dot_general | solution.py:27
  1013.1 9.8 reshape.161
  1023.0 9.5 copy.53
  1054.7 15.8 %all-reduce.14.cloned.1.call-done = (bf16[6,512,512]{2,1,0:T(8,128)(2,1)}, bf16[512,256]{1,0:T(8,128)(2,1)}, bf16[512,256]{1,0:T(8,128)(2,1)}, bf16[256,512]{1,0:T(8,128)(2,1)}) async-done(((bf16[6,512,512]{2,1,0:T(8,128)(2,1)}, bf16[512,256]{1,0:T(8,128)(2,1)}, bf16[512,256]{1,0:T(8,128)(2,1)}, bf16[256,512]{1,0:T(8,128)(2,1)}), (bf16[6,512,512]{2,1,0:T(8,128)(2,1)}, bf16[512,256]{1,0:T(8,128)(2,1)}, ...) | async-done | bytes 3932176 | tf_op jit(solution)/shard_map/psum | solution.py:179
  1081.5 142.1 %reduce-scatter.11.cloned.1.call-done = f32[128,4,512]{2,0,1:T(8,128)} async-done(((f32[1024,4,512]{2,0,1:T(8,128)}), f32[128,4,512]{2,0,1:T(8,128)}) %reduce-scatter.11.cloned.1.call-update) | async-done | bytes 1048592 | tf_op jit(solution)/shard_map/reduce_scatter | solution.py:173
  1225.3 89.7 %reduce-scatter.7.cloned.1.call-done = bf16[128,4,512]{2,0,1:T(8,128)(2,1)} async-done(((bf16[1024,4,512]{2,0,1:T(8,128)(2,1)}), bf16[128,4,512]{2,0,1:T(8,128)(2,1)}) %reduce-scatter.7.cloned.1.call-update) | async-done | bytes 524304 | tf_op jit(solution)/shard_map/reduce_scatter | solution.py:111
  1319.9 40.7 %all-reduce.7 = (f32[512]{0:T(512)}, f32[512]{0:T(512)}) all-reduce(f32[512]{0:T(512)S(1)} %get-tuple-element.38, f32[512]{0:T(512)S(1)} %copy-done.59), channel_id=1, replica_groups=mesh['rows'=4,'filt'=8] {'rows','filt'}, use_global_device_ids=true, to_apply=%region_11.12 | all-reduce | flops 1024 | bytes 8192 | tf_op jit(solution)/shard_map/psum | solution.py:184
  1360.6 97.4 %all-reduce.12.cloned.1.call-done = f32[3,512,512]{2,1,0:T(8,128)} async-done(((f32[3,512,512]{2,1,0:T(8,128)}), f32[3,512,512]{2,1,0:T(8,128)}) %all-reduce.12.cloned.1.call-update) | async-done | bytes 3145744 | tf_op jit(solution)/shard_map/psum | solution.py:184
  (257 shorter events, 450.5 us)
Async XLA Ops:
  7.2 410.4 %copy-start = (bf16[3,512,512]{2,1,0:T(8,128)(2,1)S(1)}, bf16[3,512,512]{2,1,0:T(8,128)(2,1)}, u32[]{:S(2)}) copy-start(bf16[3,512,512]{2,1,0:T(8,128)(2,1)} %param.14) | copy-start | bytes 4718596
  7.2 98.7 %all-gather.5.cloned.1.call-start = ((), (), s32[]{:S(2)}) async-start(), calls=%async_computation.4 | async-start | bytes 4718592 | tf_op jit(solution)/shard_map/all_gather | solution.py:65
  11.2 406.3 %reduce-scatter.5.cloned.1.call-start = ((), (), s32[]{:S(2)}) async-start(), calls=%async_computation.5 | async-start | bytes 9437184 | tf_op jit(solution)/shard_map/reduce_scatter | solution.py:84
  265.3 152.3 %copy-start.14 = (bf16[128,4,512]{2,1,0:T(4,128)(2,1)S(1)}, bf16[128,4,512]{2,1,0:T(4,128)(2,1)}, u32[]{:S(2)}) copy-start(bf16[128,4,512]{2,1,0:T(4,128)(2,1)} %param.10) | copy-start | bytes 1572868
  265.3 227.0 %all-gather.9.cloned.1.call-start = ((), (), s32[]{:S(2)}) async-start(), calls=%async_computation.8 | async-start | bytes 4718592 | tf_op jit(solution)/shard_map/all_gather | solution.py:119
  266.1 300.8 %all-gather.7.cloned.1.call-start = ((), (), s32[]{:S(2)}) async-start(), calls=%async_computation.6 | async-start | bytes 4718592 | tf_op jit(solution)/shard_map/all_gather | solution.py:102
  420.5 346.5 %copy-start.9 = (f32[128,4,512]{2,0,1:T(8,128)}, f32[128,4,512]{2,0,1:T(8,128)S(1)}, u32[]{:S(2)}) copy-start(f32[128,4,512]{2,0,1:T(8,128)S(1)} %get-tuple-element.61) | copy-start | bytes 3145732
  420.5 346.4 %copy-start.50 = (f32[128,4]{0,1:T(4,128)}, f32[128,4]{0,1:T(4,128)S(1)}, u32[]{:S(2)}) copy-start(f32[128,4]{0,1:T(4,128)S(1)} %add_rsqrt_fusion) | copy-start | bytes 6148
  421.6 343.1 %reduce-scatter.9.cloned.1.call-start = ((), (), s32[]{:S(2)}) async-start(), calls=%async_computation.9 | async-start | bytes 9437184 | tf_op jit(solution)/shard_map/reduce_scatter | solution.py:133
  617.0 150.5 %copy-start.20 = (bf16[128,4,512]{2,1,0:T(4,128)(2,1)S(1)}, bf16[128,4,512]{2,1,0:T(4,128)(2,1)}, u32[]{:S(2)}) copy-start(bf16[128,4,512]{2,1,0:T(4,128)(2,1)} %param.19) | copy-start | bytes 1572868
  617.0 225.4 %all-gather.11.cloned.1.call-start = ((), (), s32[]{:S(2)}) async-start(), calls=%async_computation.10 | async-start | bytes 4718592 | tf_op jit(solution)/shard_map/all_gather | solution.py:141
  769.9 300.6 %all-reduce.14.cloned.1.call-start = ((), (), s32[]{:S(2)}) async-start(), calls=%async_computation.13 | async-start | bytes 7864320 | tf_op jit(solution)/shard_map/psum | solution.py:179
  990.3 233.4 %reduce-scatter.11.cloned.1.call-start = ((), (), s32[]{:S(2)}) async-start(), calls=%async_computation.11 | async-start | bytes 9437184 | tf_op jit(solution)/shard_map/reduce_scatter | solution.py:173
  1032.5 282.5 %reduce-scatter.7.cloned.1.call-start = ((), (), s32[]{:S(2)}) async-start(), calls=%async_computation.7 | async-start | bytes 4718592 | tf_op jit(solution)/shard_map/reduce_scatter | solution.py:111
  1050.5 407.6 %all-reduce.12.cloned.1.call-start = ((), (), s32[]{:S(2)}) async-start(), calls=%async_computation.12 | async-start | bytes 6291456 | tf_op jit(solution)/shard_map/psum | solution.py:184
  1075.8 147.8 %copy-start.15 = (bf16[128,4,512]{2,1,0:T(4,128)(2,1)S(1)}, bf16[128,4,512]{2,1,0:T(4,128)(2,1)}, u32[]{:S(2)}) copy-start(bf16[128,4,512]{2,1,0:T(4,128)(2,1)} %param.10) | copy-start | bytes 1572868
  1075.8 147.8 %copy-start.53 = (f32[128,4]{0,1:T(4,128)S(1)}, f32[128,4]{0,1:T(4,128)}, u32[]{:S(2)}) copy-start(f32[128,4]{0,1:T(4,128)} %copy-done.52) | copy-start | bytes 6148
  1075.8 147.8 %copy-start.56 = (f32[512]{0:T(512)S(1)}, f32[512]{0:T(512)}, u32[]{:S(2)}) copy-start(f32[512]{0:T(512)} %param.12) | copy-start | bytes 6148
  1075.8 239.2 %copy-start.10 = (f32[128,4,512]{2,0,1:T(8,128)S(1)}, f32[128,4,512]{2,0,1:T(8,128)}, u32[]{:S(2)}) copy-start(f32[128,4,512]{2,0,1:T(8,128)} %copy-done.9) | copy-start | bytes 3145732
  1075.8 239.2 %copy-start.13 = (f32[128,4,512]{2,0,1:T(8,128)S(1)}, f32[128,4,512]{2,0,1:T(8,128)}, u32[]{:S(2)}) copy-start(f32[128,4,512]{2,0,1:T(8,128)} %reduce-scatter.9.cloned.1.call-done) | copy-start | bytes 3145732
  1075.8 239.2 %copy-start.21 = (bf16[128,4,512]{2,1,0:T(4,128)(2,1)S(1)}, bf16[128,4,512]{2,1,0:T(4,128)(2,1)}, u32[]{:S(2)}) copy-start(bf16[128,4,512]{2,1,0:T(4,128)(2,1)} %param.19) | copy-start | bytes 1572868
  1075.9 239.2 %copy-start.51 = (f32[128,4]{0,1:T(4,128)S(1)}, f32[128,4]{0,1:T(4,128)}, u32[]{:S(2)}) copy-start(f32[128,4]{0,1:T(4,128)} %copy-done.50) | copy-start | bytes 6148
  1075.9 239.2 %copy-start.55 = (f32[512]{0:T(512)S(1)}, f32[512]{0:T(512)}, u32[]{:S(2)}) copy-start(f32[512]{0:T(512)} %param.15) | copy-start | bytes 6148
  1075.9 239.2 %copy-start.58 = (f32[128,4]{0,1:T(4,128)S(1)}, f32[128,4]{0,1:T(4,128)}, u32[]{:S(2)}) copy-start(f32[128,4]{0,1:T(4,128)} %copy-done.57) | copy-start | bytes 6148
  (46 other events, 446.4 us)
Sparse Core Ops, SparseCore 0:
  11.4 76.0 all-gather.4
  265.4 152.1 reduce-scatter.4
  419.9 72.3 all-gather.8
  495.2 71.6 all-gather.6
  617.1 147.6 reduce-scatter.8
  770.0 72.3 all-gather.10
  990.4 80.0 all-reduce.13
  1074.1 149.5 reduce-scatter.10
  1227.7 87.2 reduce-scatter.6
  1320.3 137.7 all-reduce.11
where the time goes:
time: 1480 us; the launch traced here: 1470 us
  waiting for transfers between devices  785 us (53%)
  local copies, waits for them, and re-layouts  356 us (24%)
  matrix products  245 us (17%)
  blocking collectives  40.7 us (3%)
  other arithmetic  27.2 us (2%)
  between operations  15.4 us (1%)
    reduce_scatter x3, waiting for transfers between devices, shards(): lax.psum_scatter(summed.reshape(row_count, local_seqs, model_width), 'fil...  438 us
    psum x1, waiting for transfers between devices, shards(): lax.psum((regression_part, gain_in_part, gain_mid_part), ('rows', 'filt'))  97.4 us
    reduce_scatter x1, waiting for transfers between devices, shards(): lax.psum_scatter(jnp.dot(slab, w_down, preferred_element_type=jnp.float32...  89.7 us
    all_gather x1, waiting for transfers between devices, shards(): lax.all_gather(out_grad, 'filt', axis=0, tiled=True)  70.7 us
    all_gather x1, waiting for transfers between devices, shards(): lax.all_gather(middle_low, 'filt', axis=0, tiled=True)  67.2 us
    dot_general x9, matrix products, times_transpose(): lax.dot_general(left, right, (((1,), (1,)), ((), ())), preferred_element_...  65.2 us
    reshape x6, local copies, waits for them, and re-layouts, upper_toeplitz(): return tiled.reshape(seq_length, 2 * seq_length - 1)[:, :seq_length]  64.4 us
    dot_general x6, matrix products, shards(): jnp.einsum('ut,un->tn', slab, projected[project_branch], preferred_elemen...  62.5 us
  transfers between devices with their start and end apart: 10, of which 9 were waited for; matrix products, arithmetic and copies ran while one was open for 17% of the time, Pallas kernels for 0%

commit v1 on v0

--- a/solution.py
+++ b/solution.py
@@ -182,7 +182,7 @@
         lax.psum(down_partial.astype(jnp.bfloat16), "rows").astype(jnp.float32),
     )
     regression_grad, gain_in_grad, gain_mid_grad = lax.psum(
-        (regression_part, gain_in_part, gain_mid_part), ("rows", "filt")
+        lax.psum((regression_part, gain_in_part, gain_mid_part), "filt"), "rows"
     )
     return (
         block_value.astype(jnp.bfloat16),

time: 1480 us -> 1410 us (0.953)
  waiting for transfers between devices: 785 us -> 727 us
    psum x1 -> x2, waiting for transfers between devices: 97.4 us -> 38.7 us  [the longest x1 38.7 us: shards(): lax.psum(lax.psum((regression_part, gain_in_part, gain_mid_part), 'filt')...]
    psum x1 -> x2, blocking collectives: 40.7 us -> 27.3 us  [the longest x1 20.2 us: shards(): lax.psum((regression_part, gain_in_part, gain_mid_part), 'filt')]
  transfers between devices with their start and end apart: 10 -> 11, of which waited for: 9 -> 9; matrix products, arithmetic and copies ran while one was open for 17% -> 29% of each run, Pallas kernels for 0% -> 0%
where the time goes in v1:
time: 1410 us; the launch traced here: 1400 us
  waiting for transfers between devices  727 us (52%)
  local copies, waits for them, and re-layouts  355 us (25%)
  matrix products  245 us (17%)
  blocking collectives  27.3 us (2%)
  other arithmetic  27.2 us (2%)
  between operations  15.1 us (1%)
    reduce_scatter x3, waiting for transfers between devices, shards(): lax.psum_scatter(summed.reshape(row_count, local_seqs, model_width), 'fil...  439 us
    reduce_scatter x1, waiting for transfers between devices, shards(): lax.psum_scatter(jnp.dot(slab, w_down, preferred_element_type=jnp.float32...  89.1 us
    all_gather x1, waiting for transfers between devices, shards(): lax.all_gather(out_grad, 'filt', axis=0, tiled=True)  70.7 us
    all_gather x1, waiting for transfers between devices, shards(): lax.all_gather(middle_low, 'filt', axis=0, tiled=True)  67.2 us
    dot_general x9, matrix products, times_transpose(): lax.dot_general(left, right, (((1,), (1,)), ((), ())), preferred_element_...  65.1 us
    reshape x6, local copies, waits for them, and re-layouts, upper_toeplitz(): return tiled.reshape(seq_length, 2 * seq_length - 1)[:, :seq_length]  64.4 us
    dot_general x6, matrix products, shards(): jnp.einsum('ut,un->tn', slab, projected[project_branch], preferred_elemen...  62.4 us
    reshape x5, local copies, waits for them, and re-layouts, shards(): summed.reshape(row_count, local_seqs, model_width)  46.7 us
  transfers between devices with their start and end apart: 11, of which 9 were waited for; matrix products, arithmetic and copies ran while one was open for 29% of the time, Pallas kernels for 0%

profile of v1, /device:TPU:0, one launch (start us, length us, event | category | flops | bytes accessed | tf_op | source)
XLA Modules:
  0.0 1397.6 jit_solution(934171030177382052)
XLA Ops:
  17.1 10.8 reshape.145
  32.7 10.8 reshape.141
  48.4 10.7 reshape.136
  64.2 10.7 reshape.139
  79.6 10.7 reshape.147
  95.2 10.7 reshape.143
  194.6 10.8 fusion.3
  232.9 24.1 %add_add_fusion.1 = f32[1024,2048]{1,0:T(8,128)} fusion(f32[1024,2048]{1,0:T(8,128)} %fusion.3, f32[1024,2048]{1,0:T(8,128)} %fusion.6, f32[1024,2048]{1,0:T(8,128)} %fusion.9, f32[1024,2048]{1,0:T(8,128)} %fusion.15, f32[1024,2048]{1,0:T(8,128)} %fusion.12, bf16[1024,2048]{1,0:T(8,128)(2,1)} %reshape.148, bf16[1024,2047]{1,0:T(8,128)(2,1)} %reshape.147), kind=kOutput, calls=%fused_computation.2 | convolution fusion | flops 4305453056 | bytes 56623104 | tf_op jit(solution)/shard_map/ut,un->tn/dot_general | solution.py:81
  268.9 148.6 %reduce-scatter.5.cloned.1.call-done = f32[128,4,512]{2,0,1:T(8,128)} async-done(((f32[1024,4,512]{2,0,1:T(8,128)}), f32[128,4,512]{2,0,1:T(8,128)}) %reduce-scatter.5.cloned.1.call-update) | async-done | bytes 1048592 | tf_op jit(solution)/shard_map/reduce_scatter | solution.py:84
  421.5 70.7 %all-gather.9.cloned.1.call-done = bf16[1024,4,512]{2,1,0:T(4,128)(2,1)} async-done(((bf16[128,4,512]{2,1,0:T(4,128)(2,1)}), bf16[1024,4,512]{2,1,0:T(4,128)(2,1)}) %all-gather.9.cloned.1.call-update) | async-done | bytes 4194320 | tf_op jit(solution)/shard_map/all_gather | solution.py:119
  499.5 67.2 %all-gather.7.cloned.1.call-done = bf16[1024,4,512]{2,0,1:T(8,128)(2,1)} async-done(((bf16[128,4,512]{2,0,1:T(8,128)(2,1)}), bf16[1024,4,512]{2,0,1:T(8,128)(2,1)}) %all-gather.7.cloned.1.call-update) | async-done | bytes 4194320 | tf_op jit(solution)/shard_map/all_gather | solution.py:102
  597.5 10.0 reshape.152
  616.9 147.7 %reduce-scatter.9.cloned.1.call-done = f32[128,4,512]{2,0,1:T(8,128)} async-done(((f32[1024,4,512]{2,0,1:T(8,128)}), f32[128,4,512]{2,0,1:T(8,128)}) %reduce-scatter.9.cloned.1.call-update) | async-done | bytes 1048592 | tf_op jit(solution)/shard_map/reduce_scatter | solution.py:133
  815.5 12.1 copy.51
  827.6 10.3 reshape.153
  848.9 10.0 convolution_convert_fusion.7
  991.1 22.8 %add_add_fusion = f32[4096,512]{1,0:T(8,128)} fusion(f32[4096,512]{1,0:T(8,128)} %fusion.55, f32[4096,512]{1,0:T(8,128)} %fusion.58, f32[4096,512]{1,0:T(8,128)} %fusion.61, f32[4096,512]{1,0:T(8,128)} %fusion.64, f32[4096,512]{1,0:T(8,128)} %reshape.153, f32[4096,512]{1,0:T(8,128)} %fusion.67, bf16[4096,512]{1,0:T(8,128)(2,1)} %reshape.160, ...), kind=kOutput, calls=%fused_computation.1 | convolution fusion | flops 2160066560 | bytes 63438848 | tf_op jit(solution)/shard_map/dot_general | solution.py:27
  1013.9 9.8 reshape.161
  1023.8 9.5 copy.53
  1052.0 19.4 %all-reduce.18.cloned.1.call-done = (bf16[6,512,512]{2,1,0:T(8,128)(2,1)}, bf16[512,256]{1,0:T(8,128)(2,1)}, bf16[512,256]{1,0:T(8,128)(2,1)}, bf16[256,512]{1,0:T(8,128)(2,1)}) async-done(((bf16[6,512,512]{2,1,0:T(8,128)(2,1)}, bf16[512,256]{1,0:T(8,128)(2,1)}, bf16[512,256]{1,0:T(8,128)(2,1)}, bf16[256,512]{1,0:T(8,128)(2,1)}), (bf16[6,512,512]{2,1,0:T(8,128)(2,1)}, bf16[512,256]{1,0:T(8,128)(2,1)}, ...) | async-done | bytes 3932176 | tf_op jit(solution)/shard_map/psum | solution.py:179
  1082.4 142.6 %reduce-scatter.11.cloned.1.call-done = f32[128,4,512]{2,0,1:T(8,128)} async-done(((f32[1024,4,512]{2,0,1:T(8,128)}), f32[128,4,512]{2,0,1:T(8,128)}) %reduce-scatter.11.cloned.1.call-update) | async-done | bytes 1048592 | tf_op jit(solution)/shard_map/reduce_scatter | solution.py:173
  1226.7 89.1 %reduce-scatter.7.cloned.1.call-done = bf16[128,4,512]{2,0,1:T(8,128)(2,1)} async-done(((bf16[1024,4,512]{2,0,1:T(8,128)(2,1)}), bf16[128,4,512]{2,0,1:T(8,128)(2,1)}) %reduce-scatter.7.cloned.1.call-update) | async-done | bytes 524304 | tf_op jit(solution)/shard_map/reduce_scatter | solution.py:111
  1320.7 20.2 %all-reduce.7 = (f32[512]{0:T(512)S(1)}, f32[512]{0:T(512)S(1)}) all-reduce(f32[512]{0:T(512)S(1)} %get-tuple-element.38, f32[512]{0:T(512)S(1)} %copy-done.58), channel_id=1, replica_groups=mesh['rows'=4,'filt'=8] {'filt'}, use_global_device_ids=true, to_apply=%region_12.13 | all-reduce | flops 1024 | bytes 8192 | tf_op jit(solution)/shard_map/psum | solution.py:185
  1348.0 38.7 %all-reduce.16.cloned.1.call-done = f32[3,512,512]{2,1,0:T(8,128)} async-done(((f32[3,512,512]{2,1,0:T(8,128)}), f32[3,512,512]{2,1,0:T(8,128)}) %all-reduce.16.cloned.1.call-update) | async-done | bytes 3145744 | tf_op jit(solution)/shard_map/psum | solution.py:184
  (259 shorter events, 454.3 us)
Async XLA Ops:
  7.2 410.3 %copy-start = (bf16[3,512,512]{2,1,0:T(8,128)(2,1)S(1)}, bf16[3,512,512]{2,1,0:T(8,128)(2,1)}, u32[]{:S(2)}) copy-start(bf16[3,512,512]{2,1,0:T(8,128)(2,1)} %param.14) | copy-start | bytes 4718596
  7.2 98.7 %all-gather.5.cloned.1.call-start = ((), (), s32[]{:S(2)}) async-start(), calls=%async_computation.4 | async-start | bytes 4718592 | tf_op jit(solution)/shard_map/all_gather | solution.py:65
  11.2 406.2 %reduce-scatter.5.cloned.1.call-start = ((), (), s32[]{:S(2)}) async-start(), calls=%async_computation.5 | async-start | bytes 9437184 | tf_op jit(solution)/shard_map/reduce_scatter | solution.py:84
  265.1 152.3 %copy-start.14 = (bf16[128,4,512]{2,1,0:T(4,128)(2,1)S(1)}, bf16[128,4,512]{2,1,0:T(4,128)(2,1)}, u32[]{:S(2)}) copy-start(bf16[128,4,512]{2,1,0:T(4,128)(2,1)} %param.10) | copy-start | bytes 1572868
  265.1 227.1 %all-gather.9.cloned.1.call-start = ((), (), s32[]{:S(2)}) async-start(), calls=%async_computation.8 | async-start | bytes 4718592 | tf_op jit(solution)/shard_map/all_gather | solution.py:119
  265.9 300.8 %all-gather.7.cloned.1.call-start = ((), (), s32[]{:S(2)}) async-start(), calls=%async_computation.6 | async-start | bytes 4718592 | tf_op jit(solution)/shard_map/all_gather | solution.py:102
  420.3 346.5 %copy-start.9 = (f32[128,4,512]{2,0,1:T(8,128)}, f32[128,4,512]{2,0,1:T(8,128)S(1)}, u32[]{:S(2)}) copy-start(f32[128,4,512]{2,0,1:T(8,128)S(1)} %get-tuple-element.63) | copy-start | bytes 3145732
  420.3 346.5 %copy-start.49 = (f32[128,4]{0,1:T(4,128)}, f32[128,4]{0,1:T(4,128)S(1)}, u32[]{:S(2)}) copy-start(f32[128,4]{0,1:T(4,128)S(1)} %add_rsqrt_fusion) | copy-start | bytes 6148
  421.5 343.2 %reduce-scatter.9.cloned.1.call-start = ((), (), s32[]{:S(2)}) async-start(), calls=%async_computation.9 | async-start | bytes 9437184 | tf_op jit(solution)/shard_map/reduce_scatter | solution.py:133
  616.9 150.5 %copy-start.19 = (bf16[128,4,512]{2,1,0:T(4,128)(2,1)S(1)}, bf16[128,4,512]{2,1,0:T(4,128)(2,1)}, u32[]{:S(2)}) copy-start(bf16[128,4,512]{2,1,0:T(4,128)(2,1)} %param.19) | copy-start | bytes 1572868
  616.9 225.4 %all-gather.11.cloned.1.call-start = ((), (), s32[]{:S(2)}) async-start(), calls=%async_computation.10 | async-start | bytes 4718592 | tf_op jit(solution)/shard_map/all_gather | solution.py:141
  769.7 281.9 %all-reduce.14.cloned.1.call-start = ((), (), s32[]{:S(2)}) async-start(), calls=%async_computation.12 | async-start | bytes 6291456 | tf_op jit(solution)/shard_map/psum | solution.py:185
  840.6 230.7 %all-reduce.18.cloned.1.call-start = ((), (), s32[]{:S(2)}) async-start(), calls=%async_computation.14 | async-start | bytes 7864320 | tf_op jit(solution)/shard_map/psum | solution.py:179
  991.1 234.0 %reduce-scatter.11.cloned.1.call-start = ((), (), s32[]{:S(2)}) async-start(), calls=%async_computation.11 | async-start | bytes 9437184 | tf_op jit(solution)/shard_map/reduce_scatter | solution.py:173
  1033.3 282.6 %reduce-scatter.7.cloned.1.call-start = ((), (), s32[]{:S(2)}) async-start(), calls=%async_computation.7 | async-start | bytes 4718592 | tf_op jit(solution)/shard_map/reduce_scatter | solution.py:111
  1051.2 335.4 %all-reduce.16.cloned.1.call-start = ((), (), s32[]{:S(2)}) async-start(), calls=%async_computation.13 | async-start | bytes 6291456 | tf_op jit(solution)/shard_map/psum | solution.py:184
  1076.8 148.3 %copy-start.52 = (f32[128,4]{0,1:T(4,128)S(1)}, f32[128,4]{0,1:T(4,128)}, u32[]{:S(2)}) copy-start(f32[128,4]{0,1:T(4,128)} %copy-done.51) | copy-start | bytes 6148
  1076.8 148.3 %copy-start.55 = (f32[512]{0:T(512)S(1)}, f32[512]{0:T(512)}, u32[]{:S(2)}) copy-start(f32[512]{0:T(512)} %param.12) | copy-start | bytes 6148
  1076.8 239.1 %copy-start.10 = (f32[128,4,512]{2,0,1:T(8,128)S(1)}, f32[128,4,512]{2,0,1:T(8,128)}, u32[]{:S(2)}) copy-start(f32[128,4,512]{2,0,1:T(8,128)} %copy-done.9) | copy-start | bytes 3145732
  1076.8 239.1 %copy-start.13 = (f32[128,4,512]{2,0,1:T(8,128)S(1)}, f32[128,4,512]{2,0,1:T(8,128)}, u32[]{:S(2)}) copy-start(f32[128,4,512]{2,0,1:T(8,128)} %reduce-scatter.9.cloned.1.call-done) | copy-start | bytes 3145732
  1076.8 239.1 %copy-start.20 = (bf16[128,4,512]{2,1,0:T(4,128)(2,1)S(1)}, bf16[128,4,512]{2,1,0:T(4,128)(2,1)}, u32[]{:S(2)}) copy-start(bf16[128,4,512]{2,1,0:T(4,128)(2,1)} %param.19) | copy-start | bytes 1572868
  1076.8 239.0 %copy-start.50 = (f32[128,4]{0,1:T(4,128)S(1)}, f32[128,4]{0,1:T(4,128)}, u32[]{:S(2)}) copy-start(f32[128,4]{0,1:T(4,128)} %copy-done.49) | copy-start | bytes 6148
  1076.8 239.0 %copy-start.54 = (f32[512]{0:T(512)S(1)}, f32[512]{0:T(512)}, u32[]{:S(2)}) copy-start(f32[512]{0:T(512)} %param.15) | copy-start | bytes 6148
  1076.8 239.0 %copy-start.57 = (f32[128,4]{0,1:T(4,128)S(1)}, f32[128,4]{0,1:T(4,128)}, u32[]{:S(2)}) copy-start(f32[128,4]{0,1:T(4,128)} %copy-done.56) | copy-start | bytes 6148
  (46 other events, 554.0 us)
Sparse Core Ops, SparseCore 0:
  11.4 76.0 all-gather.4
  265.3 152.1 reduce-scatter.4
  419.8 72.3 all-gather.8
  495.1 71.6 all-gather.6
  617.0 147.6 reduce-scatter.8
  769.8 72.3 all-gather.10
  845.8 127.0 all-reduce.13
  991.2 80.1 all-reduce.17
  1075.5 149.5 reduce-scatter.10
  1228.5 87.2 reduce-scatter.6
  1318.3 68.2 all-reduce.15
